TPU v7x, 32 devices: a whole 2x2x4 slice. The times are simulated.
32 devices in a mesh: tm: 2 (over y), space: 16 (over z, x, core).
Axes of the slice: x: 2, y: 2, z: 4, core: 2. Of those that a mesh axis runs over, the one named last changes fastest.
Arguments:
- control: float32 [32, 51200], P(('tm', 'space')), may hold values from -4 to 4
- spectrum: float32 [51200], replicated, may hold values from 0.2 to 2
- perturb: bfloat16 [4, 32, 4, 51200], P('tm', None, None, 'space'), may hold values from -1 to 1
- obs_index: int32 [4, 32768], P('tm', 'space'), may hold values from 0 to 12799
- innovation: float32 [4, 32768], P('tm', 'space'), may hold values from -10 to 10
- obs_sigma: float32 [4, 32768], P('tm', 'space'), may hold values from 0.5 to 2
- qc_class: int32 [4, 32768], P('tm', 'space'), may hold values from 0 to 2
Outputs:
- control_out: float32 [32, 51200], P(('tm', 'space'))
- cost_list: float32 [1], replicated
Inputs may be any that keep to these rules, and one draw needn't show every extreme that they name: `obs_index`: observation o of block o // 2048 observes the cell level * 3200 + point, the point counted within the block's piece of the grid; repeats may occur.
All inputs are finite; a program needn't handle non-finite values.
Results may differ from a plain program's by a relative error of at most 0.0034.
Values may be sent and summed in bfloat16 or wider, within the bound.
A program may use at most 128 MiB of HBM per device.

v0:
```python
import functools

import jax
import jax.numpy as jnp
import ml_dtypes
import numpy as np
from jax import lax
from jax.experimental import pallas as pl
from jax.experimental.pallas import tpu as pltpu
from jax.sharding import PartitionSpec as P

GX = 320
GY = 160


def lookup_tables(segment_length):
    wave_num = jnp.arange(segment_length, dtype=jnp.float32)[:, None]
    grid_positions = jnp.arange(segment_length, dtype=jnp.float32)[None, :]
    basis = jnp.cos(jnp.pi * (grid_positions + 0.5) * wave_num / segment_length) * jnp.sqrt(
        2.0 / segment_length
    )
    return jnp.where(wave_num == 0, basis * jnp.sqrt(0.5), basis)


def synthesize(control, spectrum, basis_x, basis_y):
    coeffs = (control * spectrum[None, :]).reshape(control.shape[0], GX, GY)
    middle = jnp.einsum("kn,mkl->mnl", basis_x, coeffs, precision=lax.Precision.HIGHEST)
    result = jnp.einsum("mnl,lp->mnp", middle, basis_y, precision=lax.Precision.HIGHEST)
    return result.reshape(control.shape[0], GX * GY)


def analyze(adjoint, spectrum, basis_x, basis_y):
    state_fields = adjoint.reshape(adjoint.shape[0], GX, GY)
    middle = jnp.einsum("kn,mnp->mkp", basis_x, state_fields, precision=lax.Precision.HIGHEST)
    result = jnp.einsum("mkp,lp->mkl", middle, basis_y, precision=lax.Precision.HIGHEST)
    return result.reshape(adjoint.shape[0], GX * GY) * spectrum[None, :]


def per_device(control, spectrum, perturb, obs_index, innovation, obs_sigma, qc_class):
    basis_x = lookup_tables(GX)
    basis_y = lookup_tables(GY)
    slot_count = perturb.shape[0]
    levels = perturb.shape[2]
    piece_len = perturb.shape[3]
    radius = jnp.where(qc_class == 0, 4.0, jnp.where(qc_class == 1, 2.0, 1.0)).astype(jnp.float32)

    def scatter_cells(indices, values):
        return jnp.zeros((levels * piece_len,), jnp.float32).at[indices].add(values)

    member_field = synthesize(control, spectrum, basis_x, basis_y).astype(jnp.bfloat16)
    pieces = lax.all_to_all(member_field, "space", split_axis=1, concat_axis=0, tiled=True)
    selected_entries = perturb
    increment = jnp.einsum(
        "dzab,zb->dab",
        selected_entries,
        lax.all_gather(pieces, "tm", axis=0, tiled=True),
        preferred_element_type=jnp.float32,
    )
    cells_flat = increment.reshape(slot_count, levels * piece_len)
    modelled = jnp.take_along_axis(cells_flat, obs_index, axis=1)
    scaled = (modelled - innovation) / obs_sigma
    scaled_sq = scaled * scaled / (radius * radius)
    obs_part = jnp.sum(0.5 * radius * radius * jnp.log1p(scaled_sq))
    back_part = 0.5 * jnp.sum(control * control)
    obs_grad = scaled / ((1.0 + scaled_sq) * obs_sigma)
    control_update = jax.vmap(scatter_cells)(obs_index, obs_grad).astype(jnp.bfloat16)
    control_update = control_update.reshape(slot_count, levels, piece_len)
    selected_entries = perturb
    summed_rows = lax.psum_scatter(
        jnp.einsum(
            "qiyr,qyr->ir", selected_entries, control_update, preferred_element_type=jnp.float32
        ).astype(jnp.bfloat16),
        "tm",
        scatter_dimension=0,
        tiled=True,
    ).astype(jnp.float32)
    adjoint = lax.all_to_all(
        summed_rows.astype(jnp.bfloat16), "space", split_axis=0, concat_axis=1, tiled=True
    ).astype(summed_rows.dtype)
    gradient = control + analyze(adjoint, spectrum, basis_x, basis_y)
    grad_part = jnp.sum(gradient * gradient)
    obs_cost, back_cost = lax.psum((obs_part, back_part), ("tm", "space"))
    grad_sq = lax.psum(grad_part, ("tm", "space"))
    total_cost = back_cost + obs_cost
    step_size = 0.5 * total_cost / (grad_sq + 1e-06)
    control = control - step_size * gradient
    cost_list = [total_cost]
    return (control, jnp.stack(cost_list))


LANES = 128
FOLD = 4
MESH_ID = pl.DeviceIdType.MESH
F32 = jnp.float32
BF16 = jnp.bfloat16


def basis64(n):
    k = np.arange(n, dtype=np.float64)[:, None]
    x = np.arange(n, dtype=np.float64)[None, :]
    c = np.sqrt(2.0 / n) * np.cos(np.pi * (x + 0.5) * k / n)
    c[0] *= np.sqrt(0.5)
    return c.astype(np.float32)


def two_parts(c):
    hi = c.astype(ml_dtypes.bfloat16)
    lo = (c - hi.astype(np.float32)).astype(ml_dtypes.bfloat16)
    return np.stack([hi, lo])


def folded_bases():
    cx, cy = basis64(GX), basis64(GY)
    order = np.arange(GX).reshape(GX // FOLD, FOLD).T.reshape(-1)
    cxp = cx[order][:, order]
    return [two_parts(np.ascontiguousarray(a)) for a in (cxp, cxp.T, cy, cy.T)]


def split2(x):
    hi = x.astype(BF16)
    return hi, (x - hi.astype(F32)).astype(BF16)


def split3(x):
    a = x.astype(BF16).astype(F32)
    b = (x - a).astype(BF16).astype(F32)
    return a, b, x - a - b


def mm(a, b):
    return jnp.dot(a, b, preferred_element_type=F32)


def dot_right(x, c_ref):
    hi, lo = split2(x)
    return mm(hi, c_ref[0]) + (mm(lo, c_ref[0]) + mm(hi, c_ref[1]))


def dot_left(c_ref, x):
    hi, lo = split2(x)
    return mm(c_ref[0], hi) + (mm(c_ref[0], lo) + mm(c_ref[1], hi))


def unfold(wide):
    return jnp.concatenate([wide[:, r * GY : (r + 1) * GY] for r in range(FOLD)], axis=0)


def fold(tall):
    q = GX // FOLD
    return jnp.concatenate([tall[r * q : (r + 1) * q] for r in range(FOLD)], axis=1)


def step_kernel(
    nt, ns, n_in, *refs
):
    sources, (out, cost_out), held = refs[:n_in], refs[n_in : n_in + 2], refs[n_in + 2 :]
    landed, in_sem, held = held[:n_in], held[n_in], held[n_in + 1 :]
    control, spectrum, cy, cxpt, index, perturb, innov, sigma, qc, cxp, cyt = landed
    (
    flat, send_f, recv_f, inc, table, hi_hot, lo_hot, upd, adj_row, send_y, mid_a,
    send_a, recv_a, part, parts, grad, sf_sem, rf_sem, sr_sem, sy_sem, ry_sem, sa_sem, ra_sem, sp_sem, rp_sem,
    ) = held
    n = nt * ns
    my_t, my_s = lax.axis_index("tm"), lax.axis_index("space")
    me = my_t * ns + my_s
    slots, members, levels, piece = perturb.shape
    rows = piece // LANES
    pad_rows = send_f.shape[1]
    q, width = GX // FOLD, FOLD * GY
    tiles = width // LANES
    obs = index.shape[1]

    def peer_of(d):
        peer = lax.rem(me + d, n)
        return peer, (lax.div(peer, ns), lax.rem(peer, ns))

    loads = [
        pltpu.make_async_copy(src, dst, in_sem.at[i])
        for i, (src, dst) in enumerate(zip(sources, landed))
    ]
    for load in loads:
        load.start()

    barrier = pltpu.get_barrier_semaphore()

    def greet(d, c):
        pl.semaphore_signal(barrier, inc=1, device_id=peer_of(d)[1], device_id_type=MESH_ID)
        return c

    lax.fori_loop(1, n, greet, 0)

    def wide_of(ref):
        return jnp.concatenate(
            [ref[pl.ds(a, q, stride=tiles), :] for a in range(tiles)], axis=1
        )

    def flat_from(wide):
        for a in range(tiles):
            flat[pl.ds(a, q, stride=tiles), :] = wide[:, a * LANES : (a + 1) * LANES]

    for load in loads[:4]:
        load.wait()
    ctl = wide_of(control)
    spec = wide_of(spectrum)
    mid = dot_right(unfold(ctl * spec), cy)
    flat_from(fold(dot_left(cxpt, mid)))
    flat[q * tiles :, :] = jnp.zeros((flat.shape[0] - q * tiles, LANES), F32)
    for s in range(ns):
        send_f[s] = flat[s * rows : s * rows + pad_rows, :].astype(BF16)
    back = 0.5 * jnp.sum(ctl * ctl, axis=0, keepdims=True)
    back = sum(back[:, a * LANES : (a + 1) * LANES] for a in range(tiles))

    pl.semaphore_wait(barrier, n - 1)

    other = (nt - 1 - my_t, my_s)

    def ahead(d):
        return lax.rem(my_s + d, ns)

    def f_copy(d):
        return pltpu.make_async_remote_copy(
            send_f.at[ahead(d)], recv_f.at[me], sf_sem.at[ahead(d)], rf_sem.at[me],
            device_id=(my_t, ahead(d)), device_id_type=MESH_ID,
        )

    def relay(s):
        slot = my_t * ns + s
        return pltpu.make_async_remote_copy(
            recv_f.at[slot], recv_f.at[slot], sr_sem.at[s], rf_sem.at[slot],
            device_id=other, device_id_type=MESH_ID,
        )

    def start_f(d, c):
        f_copy(d).start()
        return c

    lax.fori_loop(1, ns, start_f, 0)
    recv_f[me] = send_f[my_s]

    loads[4].wait()
    table[...] = jnp.zeros(table.shape, F32)
    hi_rows = table.shape[1]
    his, los = [], []
    for t in range(slots):
        ix = index[t : t + 1, :]
        level, point = ix // piece, ix % piece
        hi, lo = (point // LANES) * levels + level, point % LANES
        his.append(hi)
        los.append(lo)
        hi_hot[t] = jnp.where(
            lax.broadcasted_iota(jnp.int32, (hi_rows, obs), 0) == hi, 1.0, 0.0
        ).astype(BF16)
        lo_hot[t] = jnp.where(
            lax.broadcasted_iota(jnp.int32, (LANES, obs), 0) == lo, 1.0, 0.0
        ).astype(BF16)
    inc[...] = jnp.zeros(inc.shape, F32)
    for load in loads[5:]:
        load.wait()

    def wait_f(slot):
        pltpu.make_async_remote_copy(
            send_f.at[0], recv_f.at[slot], sf_sem.at[0], rf_sem.at[slot],
            device_id=other, device_id_type=MESH_ID,
        ).wait_recv()

    relay(my_s).start()

    def pass_on(d, c):
        s = ahead(ns - d)
        wait_f(my_t * ns + s)
        relay(s).start()
        return c

    lax.fori_loop(1, ns, pass_on, 0)

    group = 8

    def add_group(g, c):
        fs = [recv_f[g * group + i].astype(F32) for i in range(group)]
        for j in range(rows):
            at = pl.ds(j * LANES, LANES)
            fb = [jnp.broadcast_to(f[j : j + 1, :], (levels, LANES)) for f in fs]
            for t in range(slots):
                total = inc[t, :, at]
                for i in range(group):
                    total = total + perturb[t, g * group + i, :, at].astype(F32) * fb[i]
                inc[t, :, at] = total
        return c

    mine, theirs = my_t * (ns // group), (nt - 1 - my_t) * (ns // group)
    lax.fori_loop(0, ns // group, lambda g, c: add_group(mine + g, c), 0)

    def add_theirs(g, c):
        for i in range(group):
            wait_f((theirs + g) * group + i)
        return add_group(theirs + g, c)

    lax.fori_loop(0, ns // group, add_theirs, 0)

    cost_row = back
    for t in range(slots):
        for j in range(rows):
            table[t, j * levels : (j + 1) * levels, :] = inc[t, :, j * LANES : (j + 1) * LANES]
        three = jnp.concatenate(split3(table[t]), axis=1).T.astype(BF16)
        picked = mm(three, hi_hot[t])
        picked = picked[:LANES] + picked[LANES : 2 * LANES] + picked[2 * LANES :]
        at_lo = lax.broadcasted_iota(jnp.int32, (LANES, obs), 0) == los[t]
        model = jnp.sum(jnp.where(at_lo, picked, 0.0), axis=0, keepdims=True)
        sg = sigma[t : t + 1, :]
        qct = qc[t : t + 1, :]
        rad = jnp.where(qct == 0, 4.0, jnp.where(qct == 1, 2.0, 1.0)).astype(F32)
        scaled = (model - innov[t : t + 1, :]) / sg
        sq = scaled * scaled / (rad * rad)
        cost = 0.5 * rad * rad * jnp.log1p(sq)
        cost_row = cost_row + sum(cost[:, a : a + LANES] for a in range(0, obs, LANES))
        g = scaled / ((1.0 + sq) * sg)
        at_hi = lax.broadcasted_iota(jnp.int32, (hi_rows, obs), 0) == his[t]
        terms = jnp.concatenate(
            [jnp.where(at_hi, p, 0.0).astype(BF16) for p in split3(g)], axis=0
        )
        u = lax.dot_general(
            terms, lo_hot[t], (((1,), (1,)), ((), ())), preferred_element_type=F32
        )
        u = u[:hi_rows] + u[hi_rows : 2 * hi_rows] + u[2 * hi_rows :]
        table[t] = u.astype(BF16).astype(F32)
        for j in range(rows):
            upd[t, :, j * LANES : (j + 1) * LANES] = table[t, j * levels : (j + 1) * levels, :]

    def y_copy(d):
        s = ahead(d)
        return pltpu.make_async_remote_copy(
            send_y.at[s], mid_a.at[s], sy_sem.at[s], ry_sem.at[s],
            device_id=other, device_id_type=MESH_ID,
        )

    def a_copy(d):
        return pltpu.make_async_remote_copy(
            send_a.at[ahead(d)], recv_a.at[my_s], sa_sem.at[ahead(d)], ra_sem.at[my_s],
            device_id=(my_t, ahead(d)), device_id_type=MESH_ID,
        )

    adj_row[...] = jnp.zeros(adj_row.shape, F32)

    def one_member(m):
        for j in range(rows):
            at = pl.ds(j * LANES, LANES)
            z = sum(perturb[t, m, :, at].astype(F32) * upd[t, :, at] for t in range(slots))
            adj_row[j : j + 1, :] = jnp.sum(z, axis=0, keepdims=True)

    def to_other(d):
        one_member((nt - 1 - my_t) * ns + ahead(d))
        send_y[ahead(d)] = adj_row[...].astype(BF16)

    def next_other(d, c):
        to_other(d)
        y_copy(d - 1).start()
        return c

    def to_owner(d):
        s = ahead(d)
        one_member(my_t * ns + s)
        y_copy(d).wait_recv()
        send_a[s] = (adj_row[...] + mid_a[s].astype(F32)).astype(BF16)

    def next_owner(d, c):
        to_owner(d)
        a_copy(d - 1).start()
        return c

    to_other(1)
    lax.fori_loop(2, ns + 1, next_other, 0)
    y_copy(ns).start()
    to_owner(1)
    lax.fori_loop(2, ns + 1, next_owner, 0)
    recv_a[my_s] = send_a[my_s]

    def wait_a(d, c):
        src = ahead(ns - d)
        pltpu.make_async_remote_copy(
            send_a.at[0], recv_a.at[src], sa_sem.at[src], ra_sem.at[src],
            device_id=(my_t, src), device_id_type=MESH_ID,
        ).wait_recv()
        return c

    lax.fori_loop(1, ns, wait_a, 0)

    for s in range(ns):
        flat[s * rows : (s + 1) * rows, :] = recv_a[s].astype(F32)[:rows]
    mid = dot_left(cxp, unfold(wide_of(flat)))
    gr = ctl + spec * fold(dot_right(mid, cyt))
    grad[...] = gr
    sq = jnp.sum(gr * gr, axis=0, keepdims=True)
    sq = sum(sq[:, a * LANES : (a + 1) * LANES] for a in range(tiles))
    part[0:1, :] = cost_row
    part[1:2, :] = sq

    def s_copy(d):
        peer, dev = peer_of(d)
        return pltpu.make_async_remote_copy(
            part, parts.at[me], sp_sem.at[peer], rp_sem.at[me],
            device_id=dev, device_id_type=MESH_ID,
        )

    def start_s(d, c):
        s_copy(d).start()
        return c

    lax.fori_loop(1, n, start_s, 0)
    parts[me] = part[...]

    def drain(d, c):
        f_copy(d).wait_send()
        a_copy(d).wait_send()
        return c

    lax.fori_loop(1, ns, drain, 0)

    def drain_y(d, c):
        relay(ahead(d)).wait_send()
        y_copy(d).wait_send()
        return c

    lax.fori_loop(1, ns + 1, drain_y, 0)

    def wait_s(d, c):
        src = lax.rem(me + n - d, n)
        pltpu.make_async_remote_copy(
            part, parts.at[src], sp_sem.at[src], rp_sem.at[src],
            device_id=(lax.div(src, ns), lax.rem(src, ns)), device_id_type=MESH_ID,
        ).wait_recv()
        return c

    lax.fori_loop(1, n, wait_s, 0)
    sums = jnp.sum(jnp.sum(parts[...], axis=0), axis=1, keepdims=True)
    total_cost, grad_sq = sums[0:1, :], sums[1:2, :]
    step = 0.5 * total_cost / (grad_sq + 1e-06)
    new = ctl - step * grad[...]
    for a in range(tiles):
        out[pl.ds(a, q, stride=tiles), :] = new[:, a * LANES : (a + 1) * LANES]
    cost_out[...] = jnp.broadcast_to(total_cost, cost_out.shape)

    def drain_s(d, c):
        s_copy(d).wait_send()
        return c

    lax.fori_loop(1, n, drain_s, 0)


def fused_device(nt, ns, control, spectrum, perturb, obs_index, innovation, obs_sigma, qc_class):
    n = nt * ns
    slots, members, levels, piece = perturb.shape
    grid_rows = GX * GY // LANES
    rows = piece // LANES
    pad_rows = -(-rows // 16) * 16
    hi_rows = -(-rows * levels // 16) * 16
    obs = obs_index.shape[1]
    vm = pl.BlockSpec(memory_space=pltpu.VMEM)
    dma = pltpu.SemaphoreType.DMA
    cxp, cxpt, cy, cyt = [jnp.asarray(b) for b in folded_bases()]
    sources = [
        control.reshape(grid_rows, LANES), spectrum.reshape(grid_rows, LANES), cy, cxpt,
        obs_index, perturb, innovation, obs_sigma, qc_class, cxp, cyt,
    ]
    out, cost = pl.pallas_call(
        functools.partial(step_kernel, nt, ns, len(sources)),
        out_shape=(
            jax.ShapeDtypeStruct((grid_rows, LANES), F32),
            jax.ShapeDtypeStruct((1, LANES), F32),
        ),
        in_specs=[pl.BlockSpec(memory_space=pltpu.HBM)] * len(sources),
        out_specs=(vm, vm),
        scratch_shapes=[
            *[pltpu.VMEM(a.shape, a.dtype) for a in sources],
            dma((len(sources),)),
            pltpu.VMEM((grid_rows + 16, LANES), F32),
            pltpu.VMEM((ns, pad_rows, LANES), BF16),
            pltpu.VMEM((n, pad_rows, LANES), BF16),
            pltpu.VMEM((slots, levels, piece), F32),
            pltpu.VMEM((slots, hi_rows, LANES), F32),
            pltpu.VMEM((slots, hi_rows, obs), BF16),
            pltpu.VMEM((slots, LANES, obs), BF16),
            pltpu.VMEM((slots, levels, piece), F32),
            pltpu.VMEM((pad_rows, LANES), F32),
            *[pltpu.VMEM((ns, pad_rows, LANES), BF16)] * 4,
            pltpu.VMEM((2, LANES), F32),
            pltpu.VMEM((n, 2, LANES), F32),
            pltpu.VMEM((GX // FOLD, FOLD * GY), F32),
            dma((ns,)), dma((n,)), *[dma((ns,))] * 5, dma((n,)), dma((n,)),
        ],
        compiler_params=pltpu.CompilerParams(
            collective_id=0, has_side_effects=True, vmem_limit_bytes=67043328
        ),
        name="envar_step",
    )(*sources)
    return out.reshape(control.shape), cost[0, :1]


def fused_fits(nt, ns, control, perturb, innovation):
    n = nt * ns
    piece = GX * GY // ns
    return (
        nt == 2
        and ns % 8 == 0
        and control.shape[0] == n
        and piece % LANES == 0
        and (FOLD * GY) % LANES == 0
        and (GX // FOLD) % 8 == 0
        and (innovation.shape[1] // ns) % LANES == 0
    )


def solution(mesh):
    nt, ns = mesh.shape["tm"], mesh.shape["space"]

    def whole(control, spectrum, perturb, obs_index, innovation, obs_sigma, qc_class):
        fits = fused_fits(nt, ns, control, perturb, innovation)
        body = functools.partial(fused_device, nt, ns) if fits else per_device
        return on_mesh(mesh, body)(
            control, spectrum, perturb, obs_index, innovation, obs_sigma, qc_class
        )

    return whole


def on_mesh(mesh, body):
    in_specs = (
        P(("tm", "space"), None),
        P(),
        P("tm", None, None, "space"),
        P("tm", "space"),
        P("tm", "space"),
        P("tm", "space"),
        P("tm", "space"),
    )
    out_specs = (P(("tm", "space"), None), P())
    return jax.shard_map(
        body, mesh=mesh, in_specs=in_specs, out_specs=out_specs, check_vma=False
    )
```

profile of v0, /device:TPU:0, one launch (start us, length us, event | category | flops | bytes accessed | tf_op | source)
XLA Modules:
  0.0 38.1 jit_solution(7588249489710537458)
XLA Ops:
  0.6 34.2 %envar_step.1 = (f32[400,128]{1,0:T(8,128)}, f32[1,128]{1,0:T(1,128)}) custom-call(f32[400,128]{1,0:T(8,128)} %bitcast.6, f32[400,128]{1,0:T(8,128)} %bitcast.7, bf16[2,160,160]{2,1,0:T(8,128)(2,1)} %constant.10.clone.refs_2_, bf16[2,320,320]{2,1,0:T(8,128)(2,1)} %constant.9.clone.refs_3_, s32[2,2048]{1,0:T(2,128)} %refs_4_.1, ...), custom_call_target="tpu_custom_call" | custom-call | tf_op jit(solution)/shard_map/envar_step/pallas_call | solution.py:464
  34.8 1.6 %copy.15 = f32[1,51200]{1,0:T(1,128)} copy(f32[1,51200]{1,0:T(1,128)} %bitcast.5) | data formatting | bytes 409600
where the time goes:
time: 38.3 us; the launch traced here: 38.1 us
  Pallas kernels  34.2 us (89%)
  between operations  2.33 us (6%)
  local copies, waits for them, and re-layouts  1.62 us (4%)
    pallas_call x1, Pallas kernels, fused_device(): pl.pallas_call(functools.partial(step_kernel, nt, ns, len(sources)), out_...  34.2 us
    unnamed x1, local copies, waits for them, and re-layouts  1.62 us

commit v1 on v0

v1 whole, which is shorter than its diff:
```python
import functools

import jax
import jax.numpy as jnp
import ml_dtypes
import numpy as np
from jax import lax
from jax.experimental import pallas as pl
from jax.experimental.pallas import tpu as pltpu
from jax.sharding import PartitionSpec as P

GX = 320
GY = 160


def lookup_tables(segment_length):
    wave_num = jnp.arange(segment_length, dtype=jnp.float32)[:, None]
    grid_positions = jnp.arange(segment_length, dtype=jnp.float32)[None, :]
    basis = jnp.cos(jnp.pi * (grid_positions + 0.5) * wave_num / segment_length) * jnp.sqrt(
        2.0 / segment_length
    )
    return jnp.where(wave_num == 0, basis * jnp.sqrt(0.5), basis)


def synthesize(control, spectrum, basis_x, basis_y):
    coeffs = (control * spectrum[None, :]).reshape(control.shape[0], GX, GY)
    middle = jnp.einsum("kn,mkl->mnl", basis_x, coeffs, precision=lax.Precision.HIGHEST)
    result = jnp.einsum("mnl,lp->mnp", middle, basis_y, precision=lax.Precision.HIGHEST)
    return result.reshape(control.shape[0], GX * GY)


def analyze(adjoint, spectrum, basis_x, basis_y):
    state_fields = adjoint.reshape(adjoint.shape[0], GX, GY)
    middle = jnp.einsum("kn,mnp->mkp", basis_x, state_fields, precision=lax.Precision.HIGHEST)
    result = jnp.einsum("mkp,lp->mkl", middle, basis_y, precision=lax.Precision.HIGHEST)
    return result.reshape(adjoint.shape[0], GX * GY) * spectrum[None, :]


def per_device(control, spectrum, perturb, obs_index, innovation, obs_sigma, qc_class):
    basis_x = lookup_tables(GX)
    basis_y = lookup_tables(GY)
    slot_count = perturb.shape[0]
    levels = perturb.shape[2]
    piece_len = perturb.shape[3]
    radius = jnp.where(qc_class == 0, 4.0, jnp.where(qc_class == 1, 2.0, 1.0)).astype(jnp.float32)

    def scatter_cells(indices, values):
        return jnp.zeros((levels * piece_len,), jnp.float32).at[indices].add(values)

    member_field = synthesize(control, spectrum, basis_x, basis_y).astype(jnp.bfloat16)
    pieces = lax.all_to_all(member_field, "space", split_axis=1, concat_axis=0, tiled=True)
    selected_entries = perturb
    increment = jnp.einsum(
        "dzab,zb->dab",
        selected_entries,
        lax.all_gather(pieces, "tm", axis=0, tiled=True),
        preferred_element_type=jnp.float32,
    )
    cells_flat = increment.reshape(slot_count, levels * piece_len)
    modelled = jnp.take_along_axis(cells_flat, obs_index, axis=1)
    scaled = (modelled - innovation) / obs_sigma
    scaled_sq = scaled * scaled / (radius * radius)
    obs_part = jnp.sum(0.5 * radius * radius * jnp.log1p(scaled_sq))
    back_part = 0.5 * jnp.sum(control * control)
    obs_grad = scaled / ((1.0 + scaled_sq) * obs_sigma)
    control_update = jax.vmap(scatter_cells)(obs_index, obs_grad).astype(jnp.bfloat16)
    control_update = control_update.reshape(slot_count, levels, piece_len)
    selected_entries = perturb
    summed_rows = lax.psum_scatter(
        jnp.einsum(
            "qiyr,qyr->ir", selected_entries, control_update, preferred_element_type=jnp.float32
        ).astype(jnp.bfloat16),
        "tm",
        scatter_dimension=0,
        tiled=True,
    ).astype(jnp.float32)
    adjoint = lax.all_to_all(
        summed_rows.astype(jnp.bfloat16), "space", split_axis=0, concat_axis=1, tiled=True
    ).astype(summed_rows.dtype)
    gradient = control + analyze(adjoint, spectrum, basis_x, basis_y)
    grad_part = jnp.sum(gradient * gradient)
    obs_cost, back_cost = lax.psum((obs_part, back_part), ("tm", "space"))
    grad_sq = lax.psum(grad_part, ("tm", "space"))
    total_cost = back_cost + obs_cost
    step_size = 0.5 * total_cost / (grad_sq + 1e-06)
    control = control - step_size * gradient
    cost_list = [total_cost]
    return (control, jnp.stack(cost_list))


LANES = 128
FOLD = 4
MESH_ID = pl.DeviceIdType.MESH
F32 = jnp.float32
BF16 = jnp.bfloat16


def basis64(n):
    k = np.arange(n, dtype=np.float64)[:, None]
    x = np.arange(n, dtype=np.float64)[None, :]
    c = np.sqrt(2.0 / n) * np.cos(np.pi * (x + 0.5) * k / n)
    c[0] *= np.sqrt(0.5)
    return c.astype(np.float32)


def two_parts(c):
    hi = c.astype(ml_dtypes.bfloat16)
    lo = (c - hi.astype(np.float32)).astype(ml_dtypes.bfloat16)
    return np.stack([hi, lo])


def folded_bases():
    cx, cy = basis64(GX), basis64(GY)
    order = np.arange(GX).reshape(GX // FOLD, FOLD).T.reshape(-1)
    cxp = cx[order][:, order]
    return [two_parts(np.ascontiguousarray(a)) for a in (cxp, cxp.T, cy, cy.T)]


def split2(x):
    hi = x.astype(BF16)
    return hi, (x - hi.astype(F32)).astype(BF16)


def split3(x):
    a = x.astype(BF16).astype(F32)
    b = (x - a).astype(BF16).astype(F32)
    return a, b, x - a - b


def mm(a, b):
    return jnp.dot(a, b, preferred_element_type=F32)


def dot_right(x, c_ref):
    hi, lo = split2(x)
    return mm(hi, c_ref[0]) + (mm(lo, c_ref[0]) + mm(hi, c_ref[1]))


def dot_left(c_ref, x):
    hi, lo = split2(x)
    return mm(c_ref[0], hi) + (mm(c_ref[0], lo) + mm(c_ref[1], hi))


def unfold(wide):
    return jnp.concatenate([wide[:, r * GY : (r + 1) * GY] for r in range(FOLD)], axis=0)


def fold(tall):
    q = GX // FOLD
    return jnp.concatenate([tall[r * q : (r + 1) * q] for r in range(FOLD)], axis=1)


def xor_of(bits, k):
    return sum(lax.rem(b + lax.rem(lax.div(k, 1 << i), 2), 2) * (1 << i) for i, b in enumerate(bits))


def gather_lanes(rows, lanes):
    return jnp.take_along_axis(rows, lanes, axis=1, mode="promise_in_bounds")


def step_kernel(nt, ns, n_in, *refs):
    sources, (out, cost_out), held = refs[:n_in], refs[n_in : n_in + 2], refs[n_in + 2 :]
    landed, in_sem, held = held[:n_in], held[n_in], held[n_in + 1 :]
    control, spectrum, cy, cxpt, index, perturb, innov, sigma, qc, cxp, cyt = landed
    (
    flat, send_f, recv_f, spread, table, hi_hot, lo_hot, upd, prod,
    send_a, recv_a, part, parts, sf_sem, rf_sem, sa_sem, ra_sem, sp_sem, rp_sem,
    ) = held
    n = nt * ns
    my_t, my_s = lax.axis_index("tm"), lax.axis_index("space")
    me = my_t * ns + my_s
    slots, levels, piece = sources[5].shape[0], sources[5].shape[2], sources[5].shape[3]
    rows = piece // LANES
    cells = rows * levels
    sent = rows + rows % 2
    pad_rows = send_f.shape[1]
    q, width = GX // FOLD, FOLD * GY
    tiles = width // LANES
    chunks = index.shape[0] // slots
    group = 8
    bits = [lax.rem(lax.div(me, 1 << i), 2) for i in range(n.bit_length() - 1)]

    def device(peer):
        return (lax.div(peer, ns), lax.rem(peer, ns))

    def peer_of(k):
        return me + sum((1 - 2 * b) * (1 << i) for i, b in enumerate(bits) if k >> i & 1)

    def load(i):
        return pltpu.make_async_copy(sources[i], landed[i], in_sem.at[i])

    for i in (0, 1, 2, 3, 4):
        load(i).start()

    barrier = pltpu.get_barrier_semaphore()

    def greet(d, c):
        peer = lax.rem(me + d, n)
        pl.semaphore_signal(barrier, inc=1, device_id=device(peer), device_id_type=MESH_ID)
        return c

    lax.fori_loop(1, n, greet, 0)

    def wide_of(ref):
        return jnp.concatenate(
            [ref[pl.ds(a, q, stride=tiles), :] for a in range(tiles)], axis=1
        )

    def flat_from(wide):
        for a in range(tiles):
            flat[pl.ds(a, q, stride=tiles), :] = wide[:, a * LANES : (a + 1) * LANES]

    for i in (0, 1, 2):
        load(i).wait()
    ctl = wide_of(control)
    spec = wide_of(spectrum)
    mid = dot_right(unfold(ctl * spec), cy)
    load(3).wait()
    flat_from(fold(dot_left(cxpt, mid)))
    flat[q * tiles :, :] = jnp.zeros((flat.shape[0] - q * tiles, LANES), F32)
    for s in range(ns):
        send_f[s] = flat[s * rows : s * rows + pad_rows, :].astype(BF16)

    pl.semaphore_wait(barrier, n - 1)

    def f_copy(k):
        peer = peer_of(k)
        t, s = device(peer)
        return pltpu.make_async_remote_copy(
            send_f.at[s, pl.ds(0, sent)], recv_f.at[me, pl.ds(0, sent)],
            sf_sem, rf_sem.at[k // group], device_id=(t, s), device_id_type=MESH_ID,
        )

    for k in range(n - 1, 0, -1):
        f_copy(k).start()
    recv_f[me] = send_f[my_s]

    for j in range(rows):
        pltpu.make_async_copy(
            sources[5].at[:, :, :, pl.ds(j * LANES, LANES)],
            perturb.at[:, :, pl.ds(j * levels, levels), :], in_sem.at[5],
        ).start()
    for i in range(6, n_in):
        load(i).start()

    back = 0.5 * jnp.sum(ctl * ctl, axis=0, keepdims=True)
    back = sum(back[:, a * LANES : (a + 1) * LANES] for a in range(tiles))
    table[...] = jnp.zeros(table.shape, F32)
    send_a[...] = jnp.zeros(send_a.shape, BF16)
    load(4).wait()
    hi_rows, lo_cols = hi_hot.shape[1], lo_hot.shape[2]
    his, los = [], []
    for t in range(slots):
        ix = index[pl.ds(t, chunks, stride=slots), :]
        level, point = ix // piece, ix % piece
        hi, lo = (point // LANES) * levels + level, point % LANES
        his.append(hi)
        los.append(lo)
        row = (hi // 16) * 8 + hi % 8
        col = (((hi // 8) % 2) * LANES + lo).T
        for c in range(chunks):
            at = pl.ds(c * LANES, LANES)
            hi_hot[t, :, at] = jnp.where(
                lax.broadcasted_iota(jnp.int32, (hi_rows, LANES), 0) == row[c : c + 1, :], 1.0, 0.0
            ).astype(BF16)
            lo_hot[t, at, :] = jnp.where(
                lax.broadcasted_iota(jnp.int32, (LANES, lo_cols), 1) == col[:, c : c + 1], 1.0, 0.0
            ).astype(BF16)
    whole = perturb.at[:, :, pl.ds(0, cells), :]
    pltpu.make_async_copy(whole, whole, in_sem.at[5]).wait()

    my_block = lax.div(me, group)
    block_bits = bits[group.bit_length() - 1 :]

    def add_group(g, own):
        block = xor_of(block_bits, g)
        arrived = recv_f.at[pl.ds(0, group - own), pl.ds(0, sent)]
        pltpu.make_async_copy(arrived, arrived, rf_sem.at[g]).wait()
        for i in range(group):
            f = recv_f[block * group + i].astype(F32)[:rows]
            for l in range(levels):
                spread[i, pl.ds(l, rows, stride=levels), :] = f
        for t in range(slots):
            total = table[t, pl.ds(0, cells), :]
            for i in range(group):
                p = perturb[t, block * group + i, pl.ds(0, cells), :].astype(F32)
                total = total + p * spread[i, pl.ds(0, cells), :]
            table[t, pl.ds(0, cells), :] = total

    add_group(0, 1)
    n_groups = n // group

    def next_group(i, c):
        g = lax.rem(2 * i, n_groups) + lax.div(2 * i, n_groups)
        add_group(g, 0)
        return c

    lax.fori_loop(1, n_groups, next_group, 0)

    for i in (6, 7, 8):
        load(i).wait()
    costs = []
    for t in range(slots):
        model = jnp.zeros((chunks, LANES), F32)
        for h in range(cells):
            picked = gather_lanes(jnp.broadcast_to(table[t, h : h + 1, :], (chunks, LANES)), los[t])
            model = jnp.where(his[t] == h, picked, model)
        mine = pl.ds(t, chunks, stride=slots)
        sg = sigma[mine, :]
        qct = qc[mine, :]
        rad = jnp.where(qct == 0, 4.0, jnp.where(qct == 1, 2.0, 1.0)).astype(F32)
        scaled = (model - innov[mine, :]) / sg
        sq = scaled * scaled / (rad * rad)
        costs.append((rad, sq))
        g = scaled / ((1.0 + sq) * sg)
        terms = jnp.concatenate(
            [
                hi_hot[t, :, c * LANES : (c + 1) * LANES]
                * jnp.broadcast_to(g[c : c + 1, :], (hi_rows, LANES)).astype(BF16)
                for c in range(chunks)
            ],
            axis=1,
        )
        u = mm(terms, lo_hot[t]).astype(BF16).astype(F32)
        for b in range(upd.shape[1] // 8):
            upd[t, b * 8 : (b + 1) * 8, :] = u[
                (b // 2) * 8 : (b // 2 + 1) * 8, (b % 2) * LANES : (b % 2 + 1) * LANES
            ]

    def a_copy(peer):
        return pltpu.make_async_remote_copy(
            send_a.at[peer, pl.ds(0, sent)], recv_a.at[me, pl.ds(0, sent)], sa_sem, ra_sem,
            device_id=device(peer), device_id_type=MESH_ID,
        )

    def one_member(m, to):
        prod[pl.ds(0, cells), :] = sum(
            perturb[t, m, pl.ds(0, cells), :].astype(F32) * upd[t, pl.ds(0, cells), :]
            for t in range(slots)
        )
        to[pl.ds(0, rows), :] = sum(
            prod[pl.ds(l, rows, stride=levels), :] for l in range(levels)
        ).astype(BF16)

    def next_member(i, before):
        peer = xor_of(bits, n - 1 - i)
        one_member(peer, send_a.at[peer])
        a_copy(before).start()
        return peer

    first = peer_of(n - 1)
    one_member(first, send_a.at[first])
    last = lax.fori_loop(1, n - 1, next_member, first)
    one_member(me, recv_a.at[me])
    a_copy(last).start()

    cost_row = back
    for rad, sq in costs:
        cost_row = cost_row + jnp.sum(0.5 * rad * rad * jnp.log1p(sq), axis=0, keepdims=True)
    part[0:1, :] = cost_row
    for i in (9, 10):
        load(i).wait()

    others = recv_a.at[pl.ds(0, n - 1), pl.ds(0, sent)]
    pltpu.make_async_copy(others, others, ra_sem).wait()
    for s in range(ns):
        flat[s * rows : (s + 1) * rows, :] = sum(
            recv_a[t * ns + s].astype(F32)[:rows] for t in range(nt)
        )
    mid = dot_left(cxp, unfold(wide_of(flat)))
    gr = ctl + spec * fold(dot_right(mid, cyt))
    sq = jnp.sum(gr * gr, axis=0, keepdims=True)
    part[1:2, :] = sum(sq[:, a * LANES : (a + 1) * LANES] for a in range(tiles))

    def s_copy(k):
        peer = peer_of(k)
        return pltpu.make_async_remote_copy(
            part, parts.at[me], sp_sem, rp_sem, device_id=device(peer), device_id_type=MESH_ID,
        )

    for k in range(n - 1, 0, -1):
        s_copy(k).start()
    parts[me] = part[...]
    flat_from(gr)
    all_sent = send_a.at[pl.ds(0, n - 1), pl.ds(0, sent)]
    pltpu.make_async_copy(all_sent, all_sent, sf_sem).wait()
    pltpu.make_async_copy(all_sent, all_sent, sa_sem).wait()

    all_parts = parts.at[pl.ds(0, n - 1)]
    pltpu.make_async_copy(all_parts, all_parts, sp_sem).wait()
    pltpu.make_async_copy(all_parts, all_parts, rp_sem).wait()
    sums = jnp.sum(jnp.sum(parts[...], axis=0), axis=1, keepdims=True)
    total_cost, grad_sq = sums[0:1, :], sums[1:2, :]
    step = 0.5 * total_cost / (grad_sq + 1e-06)
    out[...] = control[...] - step * flat[: q * tiles, :]
    cost_out[...] = jnp.broadcast_to(total_cost, cost_out.shape)


def fused_device(nt, ns, control, spectrum, perturb, obs_index, innovation, obs_sigma, qc_class):
    n = nt * ns
    slots, members, levels, piece = perturb.shape
    grid_rows = GX * GY // LANES
    rows = piece // LANES
    cells = rows * levels
    pad_rows = -(-rows // 16) * 16
    pad_cells = -(-cells // 16) * 16
    hi_rows = -(-cells // 32) * 16
    obs = obs_index.shape[1]
    vm = pl.BlockSpec(memory_space=pltpu.VMEM)
    dma = pltpu.SemaphoreType.DMA
    cxp, cxpt, cy, cyt = [jnp.asarray(b) for b in folded_bases()]

    def by_chunk(x):
        return x.reshape(slots, obs // LANES, LANES).transpose(1, 0, 2).reshape(-1, LANES)

    sources = [
        control.reshape(grid_rows, LANES), spectrum.reshape(grid_rows, LANES), cy, cxpt,
        by_chunk(obs_index), perturb, by_chunk(innovation), by_chunk(obs_sigma),
        by_chunk(qc_class), cxp, cyt,
    ]
    lands = [pltpu.VMEM(a.shape, a.dtype) for a in sources]
    lands[5] = pltpu.VMEM((slots, members, pad_cells, LANES), BF16)
    out, cost = pl.pallas_call(
        functools.partial(step_kernel, nt, ns, len(sources)),
        out_shape=(
            jax.ShapeDtypeStruct((grid_rows, LANES), F32),
            jax.ShapeDtypeStruct((1, LANES), F32),
        ),
        in_specs=[pl.BlockSpec(memory_space=pltpu.HBM)] * len(sources),
        out_specs=(vm, vm),
        scratch_shapes=[
            *lands,
            dma((len(sources),)),
            pltpu.VMEM((grid_rows + 16, LANES), F32),
            pltpu.VMEM((ns, pad_rows, LANES), BF16),
            pltpu.VMEM((n, pad_rows, LANES), BF16),
            pltpu.VMEM((8, pad_cells, LANES), F32),
            pltpu.VMEM((slots, pad_cells, LANES), F32),
            pltpu.VMEM((slots, hi_rows, obs), BF16),
            pltpu.VMEM((slots, obs, 2 * LANES), BF16),
            pltpu.VMEM((slots, -(-cells // 8) * 8, LANES), F32),
            pltpu.VMEM((pad_cells, LANES), F32),
            pltpu.VMEM((n, pad_rows, LANES), BF16),
            pltpu.VMEM((n, pad_rows, LANES), BF16),
            pltpu.VMEM((2, LANES), F32),
            pltpu.VMEM((n, 2, LANES), F32),
            dma, dma((n // 8,)), dma, dma, dma, dma,
        ],
        compiler_params=pltpu.CompilerParams(
            collective_id=0, has_side_effects=True, vmem_limit_bytes=24 << 20
        ),
        name="envar_step",
    )(*[pltpu.with_memory_space_constraint(a, pltpu.HBM) for a in sources])
    return out.reshape(control.shape), cost[0, :1]


def fused_fits(nt, ns, control, perturb, innovation):
    n = nt * ns
    piece = GX * GY // ns
    return (
        nt == 2
        and ns == 16
        and control.shape[0] == n
        and perturb.shape[2] == 4
        and piece % LANES == 0
        and (FOLD * GY) % LANES == 0
        and (GX // FOLD) % 8 == 0
        and innovation.shape[1] // ns == 16 * LANES
    )


def solution(mesh):
    nt, ns = mesh.shape["tm"], mesh.shape["space"]

    def whole(control, spectrum, perturb, obs_index, innovation, obs_sigma, qc_class):
        fits = fused_fits(nt, ns, control, perturb, innovation)
        body = functools.partial(fused_device, nt, ns) if fits else per_device
        return on_mesh(mesh, body)(
            control, spectrum, perturb, obs_index, innovation, obs_sigma, qc_class
        )

    return whole


def on_mesh(mesh, body):
    in_specs = (
        P(("tm", "space"), None),
        P(),
        P("tm", None, None, "space"),
        P("tm", "space"),
        P("tm", "space"),
        P("tm", "space"),
        P("tm", "space"),
    )
    out_specs = (P(("tm", "space"), None), P())
    return jax.shard_map(
        body, mesh=mesh, in_specs=in_specs, out_specs=out_specs, check_vma=False
    )
```

time: 38.3 us -> 29.5 us (0.77)
  Pallas kernels: 34.2 us -> 26.9 us
  local copies, waits for them, and re-layouts: 1.62 us -> 0.68 us
  between operations: 2.33 us -> 1.81 us
    pallas_call x1, Pallas kernels: 34.2 us -> 26.9 us  [fused_device(): pl.pallas_call(functools.partial(step_kernel, nt, ns, len(sources)), out_...]
    unnamed x1, local copies, waits for them, and re-layouts: 1.62 us -> 0.68 us
where the time goes in v1:
time: 29.5 us; the launch traced here: 29.4 us
  Pallas kernels  26.9 us (91%)
  between operations  1.81 us (6%)
  local copies, waits for them, and re-layouts  0.68 us (2%)
    pallas_call x1, Pallas kernels, fused_device(): pl.pallas_call(functools.partial(step_kernel, nt, ns, len(sources)), out_...  26.9 us
    unnamed x1, local copies, waits for them, and re-layouts  0.68 us

profile of v1, /device:TPU:0, one launch (start us, length us, event | category | flops | bytes accessed | tf_op | source)
XLA Modules:
  0.0 29.4 jit_solution(17513208990094491727)
XLA Ops:
  0.6 26.9 %envar_step.1 = (f32[400,128]{1,0:T(8,128)S(1)}, f32[1,128]{1,0:T(1,128)S(1)}) custom-call(f32[400,128]{1,0:T(8,128)} %bitcast.27, f32[400,128]{1,0:T(8,128)} %bitcast.28, bf16[2,160,160]{2,1,0:T(8,128)(2,1)} %constant.10.clone.refs_2_, bf16[2,320,320]{2,1,0:T(8,128)(2,1)} %constant.9.clone.refs_3_, s32[32,128]{1,0:T(8,128)} %bitcast.29, ...), custom_call_target="tpu_custom_call" | custom-call | tf_op jit(solution)/shard_map/envar_step/pallas_call | solution.py:423
  27.5 0.7 %copy.19 = f32[1,51200]{1,0:T(1,128)} copy(f32[1,51200]{1,0:T(1,128)S(1)} %bitcast.25) | data formatting | bytes 409600

commit v2 on v1

--- a/solution.py
+++ b/solution.py
@@ -103,42 +103,15 @@
     return c.astype(np.float32)
 
 
-def two_parts(c):
-    hi = c.astype(ml_dtypes.bfloat16)
-    lo = (c - hi.astype(np.float32)).astype(ml_dtypes.bfloat16)
-    return np.stack([hi, lo])
-
-
 def folded_bases():
     cx, cy = basis64(GX), basis64(GY)
     order = np.arange(GX).reshape(GX // FOLD, FOLD).T.reshape(-1)
     cxp = cx[order][:, order]
-    return [two_parts(np.ascontiguousarray(a)) for a in (cxp, cxp.T, cy, cy.T)]
-
-
-def split2(x):
-    hi = x.astype(BF16)
-    return hi, (x - hi.astype(F32)).astype(BF16)
-
-
-def split3(x):
-    a = x.astype(BF16).astype(F32)
-    b = (x - a).astype(BF16).astype(F32)
-    return a, b, x - a - b
+    return [np.ascontiguousarray(a).astype(ml_dtypes.bfloat16) for a in (cxp, cxp.T, cy, cy.T)]
 
 
 def mm(a, b):
     return jnp.dot(a, b, preferred_element_type=F32)
-
-
-def dot_right(x, c_ref):
-    hi, lo = split2(x)
-    return mm(hi, c_ref[0]) + (mm(lo, c_ref[0]) + mm(hi, c_ref[1]))
-
-
-def dot_left(c_ref, x):
-    hi, lo = split2(x)
-    return mm(c_ref[0], hi) + (mm(c_ref[0], lo) + mm(c_ref[1], hi))
 
 
 def unfold(wide):
@@ -194,12 +167,10 @@
 
     barrier = pltpu.get_barrier_semaphore()
 
-    def greet(d, c):
-        peer = lax.rem(me + d, n)
-        pl.semaphore_signal(barrier, inc=1, device_id=device(peer), device_id_type=MESH_ID)
-        return c
-
-    lax.fori_loop(1, n, greet, 0)
+    for k in range(n - 1, 0, -1):
+        pl.semaphore_signal(
+            barrier, inc=1, device_id=device(peer_of(k)), device_id_type=MESH_ID
+        )
 
     def wide_of(ref):
         return jnp.concatenate(
@@ -214,9 +185,9 @@
         load(i).wait()
     ctl = wide_of(control)
     spec = wide_of(spectrum)
-    mid = dot_right(unfold(ctl * spec), cy)
+    mid = mm(unfold((ctl * spec).astype(BF16)), cy[...]).astype(BF16)
     load(3).wait()
-    flat_from(fold(dot_left(cxpt, mid)))
+    flat_from(fold(mm(cxpt[...], mid)))
     flat[q * tiles :, :] = jnp.zeros((flat.shape[0] - q * tiles, LANES), F32)
     for s in range(ns):
         send_f[s] = flat[s * rows : s * rows + pad_rows, :].astype(BF16)
@@ -367,8 +338,8 @@
         flat[s * rows : (s + 1) * rows, :] = sum(
             recv_a[t * ns + s].astype(F32)[:rows] for t in range(nt)
         )
-    mid = dot_left(cxp, unfold(wide_of(flat)))
-    gr = ctl + spec * fold(dot_right(mid, cyt))
+    mid = mm(cxp[...], unfold(wide_of(flat).astype(BF16))).astype(BF16)
+    gr = ctl + spec * fold(mm(mid, cyt[...]))
     sq = jnp.sum(gr * gr, axis=0, keepdims=True)
     part[1:2, :] = sum(sq[:, a * LANES : (a + 1) * LANES] for a in range(tiles))
 
@@ -394,6 +365,17 @@
     step = 0.5 * total_cost / (grad_sq + 1e-06)
     out[...] = control[...] - step * flat[: q * tiles, :]
     cost_out[...] = jnp.broadcast_to(total_cost, cost_out.shape)
+
+
+def put_kernel(out, cost, out_to, cost_to, sem):
+    copies = [
+        pltpu.make_async_copy(src, dst, sem.at[i])
+        for i, (src, dst) in enumerate(((out, out_to), (cost, cost_to)))
+    ]
+    for copy in copies:
+        copy.start()
+    for copy in copies:
+        copy.wait()
 
 
 def fused_device(nt, ns, control, spectrum, perturb, obs_index, innovation, obs_sigma, qc_class):
@@ -451,6 +433,17 @@
         ),
         name="envar_step",
     )(*[pltpu.with_memory_space_constraint(a, pltpu.HBM) for a in sources])
+    out, cost = pl.pallas_call(
+        put_kernel,
+        out_shape=(
+            jax.ShapeDtypeStruct((grid_rows, LANES), F32),
+            jax.ShapeDtypeStruct((1, LANES), F32),
+        ),
+        in_specs=[pl.BlockSpec(memory_space=pltpu.VMEM)] * 2,
+        out_specs=[pl.BlockSpec(memory_space=pltpu.HBM)] * 2,
+        scratch_shapes=[dma((2,))],
+        name="put_results",
+    )(*[pltpu.with_memory_space_constraint(a, pltpu.VMEM) for a in (out, cost)])
     return out.reshape(control.shape), cost[0, :1]
 
 

time: 29.5 us -> 27.8 us (0.942)
  between operations: 1.81 us -> 0.64 us
  local copies, waits for them, and re-layouts: 0.68 us -> 0 us
    pallas_call x0 -> x1, Pallas kernels: none -> 0.7 us  [fused_device(): pl.pallas_call(put_kernel, out_shape=(jax.ShapeDtypeStruct((grid_rows, LA...]
    unnamed x1 -> x0, local copies, waits for them, and re-layouts: 0.68 us -> none
    pallas_call x1, Pallas kernels: 26.9 us -> 26.3 us  [fused_device(): pl.pallas_call(functools.partial(step_kernel, nt, ns, len(sources)), out_...]
where the time goes in v2:
time: 27.8 us; the launch traced here: 27.6 us
  Pallas kernels  27 us (97%)
  between operations  0.64 us (2%)
    pallas_call x1, Pallas kernels, fused_device(): pl.pallas_call(functools.partial(step_kernel, nt, ns, len(sources)), out_...  26.3 us
    pallas_call x1, Pallas kernels, fused_device(): pl.pallas_call(put_kernel, out_shape=(jax.ShapeDtypeStruct((grid_rows, LA...  0.7 us

profile of v2, /device:TPU:0, one launch (start us, length us, event | category | flops | bytes accessed | tf_op | source)
XLA Modules:
  0.0 27.6 jit_solution(15517716688593763333)
XLA Ops:
  0.6 26.3 %envar_step.1 = (f32[400,128]{1,0:T(8,128)S(1)}, f32[1,128]{1,0:T(1,128)S(1)}) custom-call(f32[400,128]{1,0:T(8,128)} %bitcast.25, f32[400,128]{1,0:T(8,128)} %bitcast.26, bf16[160,160]{1,0:T(8,128)(2,1)} %constant.10.clone.refs_2_, bf16[320,320]{1,0:T(8,128)(2,1)} %constant.9.clone.refs_3_, s32[32,128]{1,0:T(8,128)} %bitcast.27, ...), custom_call_target="tpu_custom_call" | custom-call | tf_op jit(solution)/shard_map/envar_step/pallas_call | solution.py:405
  26.9 0.7 %put_results.1 = (f32[400,128]{1,0:T(8,128)}, f32[1,128]{1,0:T(1,128)}) custom-call(f32[400,128]{1,0:T(8,128)S(1)} %get-tuple-element.6.out, f32[1,128]{1,0:T(1,128)S(1)} %get-tuple-element.7.cost), custom_call_target="tpu_custom_call" | custom-call | tf_op jit(solution)/shard_map/put_results/pallas_call | solution.py:436

commit v3 on v2

--- a/solution.py
+++ b/solution.py
@@ -152,6 +152,8 @@
     chunks = index.shape[0] // slots
     group = 8
     bits = [lax.rem(lax.div(me, 1 << i), 2) for i in range(n.bit_length() - 1)]
+    n_groups = n // group
+    ranges = [(16, rows - 16, sent - 16), (0, 16, 16)] if rows > 16 else [(0, rows, sent)]
 
     def device(peer):
         return (lax.div(peer, ns), lax.rem(peer, ns))
@@ -194,16 +196,18 @@
 
     pl.semaphore_wait(barrier, n - 1)
 
-    def f_copy(k):
+    def f_copy(p, k):
         peer = peer_of(k)
         t, s = device(peer)
+        at = pl.ds(ranges[p][0], ranges[p][2])
         return pltpu.make_async_remote_copy(
-            send_f.at[s, pl.ds(0, sent)], recv_f.at[me, pl.ds(0, sent)],
-            sf_sem, rf_sem.at[k // group], device_id=(t, s), device_id_type=MESH_ID,
-        )
-
-    for k in range(n - 1, 0, -1):
-        f_copy(k).start()
+            send_f.at[s, at], recv_f.at[me, at], sf_sem, rf_sem.at[p * n_groups + k // group],
+            device_id=(t, s), device_id_type=MESH_ID,
+        )
+
+    for p in range(len(ranges)):
+        for k in range(n - 1, 0, -1):
+            f_copy(p, k).start()
     recv_f[me] = send_f[my_s]
 
     for j in range(rows):
@@ -227,12 +231,11 @@
         hi, lo = (point // LANES) * levels + level, point % LANES
         his.append(hi)
         los.append(lo)
-        row = (hi // 16) * 8 + hi % 8
-        col = (((hi // 8) % 2) * LANES + lo).T
+        col = lo.T
         for c in range(chunks):
             at = pl.ds(c * LANES, LANES)
             hi_hot[t, :, at] = jnp.where(
-                lax.broadcasted_iota(jnp.int32, (hi_rows, LANES), 0) == row[c : c + 1, :], 1.0, 0.0
+                lax.broadcasted_iota(jnp.int32, (hi_rows, LANES), 0) == hi[c : c + 1, :], 1.0, 0.0
             ).astype(BF16)
             lo_hot[t, at, :] = jnp.where(
                 lax.broadcasted_iota(jnp.int32, (LANES, lo_cols), 1) == col[:, c : c + 1], 1.0, 0.0
@@ -240,90 +243,114 @@
     whole = perturb.at[:, :, pl.ds(0, cells), :]
     pltpu.make_async_copy(whole, whole, in_sem.at[5]).wait()
 
-    my_block = lax.div(me, group)
     block_bits = bits[group.bit_length() - 1 :]
 
-    def add_group(g, own):
+    def add_group(p, g, own):
+        r0, real, wide = ranges[p]
+        at = pl.ds(r0 * levels, real * levels)
         block = xor_of(block_bits, g)
-        arrived = recv_f.at[pl.ds(0, group - own), pl.ds(0, sent)]
-        pltpu.make_async_copy(arrived, arrived, rf_sem.at[g]).wait()
+        arrived = recv_f.at[pl.ds(0, group - own), pl.ds(0, wide)]
+        pltpu.make_async_copy(arrived, arrived, rf_sem.at[p * n_groups + g]).wait()
         for i in range(group):
-            f = recv_f[block * group + i].astype(F32)[:rows]
+            f = recv_f[block * group + i, r0:, :].astype(F32)[:real]
             for l in range(levels):
-                spread[i, pl.ds(l, rows, stride=levels), :] = f
+                spread[i, pl.ds(r0 * levels + l, real, stride=levels), :] = f
         for t in range(slots):
-            total = table[t, pl.ds(0, cells), :]
+            total = table[t, at, :]
             for i in range(group):
-                p = perturb[t, block * group + i, pl.ds(0, cells), :].astype(F32)
-                total = total + p * spread[i, pl.ds(0, cells), :]
-            table[t, pl.ds(0, cells), :] = total
-
-    add_group(0, 1)
-    n_groups = n // group
-
-    def next_group(i, c):
-        g = lax.rem(2 * i, n_groups) + lax.div(2 * i, n_groups)
-        add_group(g, 0)
-        return c
-
-    lax.fori_loop(1, n_groups, next_group, 0)
-
-    for i in (6, 7, 8):
-        load(i).wait()
-    costs = []
-    for t in range(slots):
-        model = jnp.zeros((chunks, LANES), F32)
-        for h in range(cells):
-            picked = gather_lanes(jnp.broadcast_to(table[t, h : h + 1, :], (chunks, LANES)), los[t])
-            model = jnp.where(his[t] == h, picked, model)
-        mine = pl.ds(t, chunks, stride=slots)
-        sg = sigma[mine, :]
-        qct = qc[mine, :]
-        rad = jnp.where(qct == 0, 4.0, jnp.where(qct == 1, 2.0, 1.0)).astype(F32)
-        scaled = (model - innov[mine, :]) / sg
-        sq = scaled * scaled / (rad * rad)
-        costs.append((rad, sq))
-        g = scaled / ((1.0 + sq) * sg)
-        terms = jnp.concatenate(
-            [
-                hi_hot[t, :, c * LANES : (c + 1) * LANES]
-                * jnp.broadcast_to(g[c : c + 1, :], (hi_rows, LANES)).astype(BF16)
-                for c in range(chunks)
-            ],
-            axis=1,
-        )
-        u = mm(terms, lo_hot[t]).astype(BF16).astype(F32)
-        for b in range(upd.shape[1] // 8):
-            upd[t, b * 8 : (b + 1) * 8, :] = u[
-                (b // 2) * 8 : (b // 2 + 1) * 8, (b % 2) * LANES : (b % 2 + 1) * LANES
-            ]
-
-    def a_copy(peer):
+                v = perturb[t, block * group + i, at, :].astype(F32)
+                total = total + v * spread[i, at, :]
+            table[t, at, :] = total
+
+    def increments(p):
+        add_group(p, 0, 1)
+
+        def next_group(i, c):
+            g = lax.rem(2 * i, n_groups) + lax.div(2 * i, n_groups)
+            add_group(p, g, 0)
+            return c
+
+        lax.fori_loop(1, n_groups, next_group, 0)
+
+    models = [jnp.zeros((chunks, LANES), F32) for t in range(slots)]
+    costs = [None] * slots
+
+    def observe(p):
+        r0, real, wide = ranges[p]
+        top = hi_rows if r0 + real == rows else (r0 + real) * levels
+        for t in range(slots):
+            for h in range(r0 * levels, (r0 + real) * levels):
+                picked = gather_lanes(
+                    jnp.broadcast_to(table[t, h : h + 1, :], (chunks, LANES)), los[t]
+                )
+                models[t] = jnp.where(his[t] == h, picked, models[t])
+            mine = pl.ds(t, chunks, stride=slots)
+            sg = sigma[mine, :]
+            qct = qc[mine, :]
+            rad = jnp.where(qct == 0, 4.0, jnp.where(qct == 1, 2.0, 1.0)).astype(F32)
+            scaled = (models[t] - innov[mine, :]) / sg
+            sq = scaled * scaled / (rad * rad)
+            costs[t] = (rad, sq)
+            g = scaled / ((1.0 + sq) * sg)
+            terms = jnp.concatenate(
+                [
+                    hi_hot[t, r0 * levels : top, c * LANES : (c + 1) * LANES]
+                    * jnp.broadcast_to(g[c : c + 1, :], (top - r0 * levels, LANES)).astype(BF16)
+                    for c in range(chunks)
+                ],
+                axis=1,
+            )
+            upd[t, r0 * levels : top, :] = mm(terms, lo_hot[t]).astype(BF16).astype(F32)
+
+    def a_copy(p, peer):
+        at = pl.ds(ranges[p][0], ranges[p][2])
         return pltpu.make_async_remote_copy(
-            send_a.at[peer, pl.ds(0, sent)], recv_a.at[me, pl.ds(0, sent)], sa_sem, ra_sem,
+            send_a.at[peer, at], recv_a.at[me, at], sa_sem, ra_sem,
             device_id=device(peer), device_id_type=MESH_ID,
         )
 
-    def one_member(m, to):
-        prod[pl.ds(0, cells), :] = sum(
-            perturb[t, m, pl.ds(0, cells), :].astype(F32) * upd[t, pl.ds(0, cells), :]
-            for t in range(slots)
-        )
-        to[pl.ds(0, rows), :] = sum(
-            prod[pl.ds(l, rows, stride=levels), :] for l in range(levels)
+    def one_member(p, m, i, to):
+        r0, real, wide = ranges[p]
+        at = pl.ds(r0 * levels, real * levels)
+        prod[i, at, :] = sum(
+            perturb[t, m, at, :].astype(F32) * upd[t, at, :] for t in range(slots)
+        )
+        to[pl.ds(r0, real), :] = sum(
+            prod[i, pl.ds(r0 * levels + l, real, stride=levels), :] for l in range(levels)
         ).astype(BF16)
 
-    def next_member(i, before):
-        peer = xor_of(bits, n - 1 - i)
-        one_member(peer, send_a.at[peer])
-        a_copy(before).start()
-        return peer
-
-    first = peer_of(n - 1)
-    one_member(first, send_a.at[first])
-    last = lax.fori_loop(1, n - 1, next_member, first)
-    one_member(me, recv_a.at[me])
-    a_copy(last).start()
+    def low_of(i):
+        return sum((1 - 2 * b) * (1 << j) for j, b in enumerate(bits[:3]) if i >> j & 1)
+
+    def adjoints(p):
+        def eight(d, before):
+            base = xor_of(block_bits, n_groups - 1 - d) * group + lax.rem(me, group)
+            for i in range(group - 1, -1, -1):
+                peer = base + low_of(i)
+                one_member(p, peer, i, send_a.at[peer])
+                if i < group - 1:
+                    a_copy(p, base + low_of(i + 1)).start()
+            return base
+
+        def next_eight(d, before):
+            a_copy(p, before).start()
+            return eight(d, before)
+
+        last = lax.fori_loop(1, n_groups - 1, next_eight, eight(0, 0))
+        for i in range(group - 1, 0, -1):
+            peer = peer_of(i)
+            one_member(p, peer, i, send_a.at[peer])
+            a_copy(p, last if i == group - 1 else peer_of(i + 1)).start()
+        one_member(p, me, 0, recv_a.at[me])
+        a_copy(p, peer_of(1)).start()
+
+    for p in range(len(ranges)):
+        increments(p)
+        if p == 0:
+            for i in (6, 7, 8):
+                load(i).wait()
+        observe(p)
+        adjoints(p)
 
     cost_row = back
     for rad, sq in costs:
@@ -386,7 +413,7 @@
     cells = rows * levels
     pad_rows = -(-rows // 16) * 16
     pad_cells = -(-cells // 16) * 16
-    hi_rows = -(-cells // 32) * 16
+    hi_rows = pad_cells
     obs = obs_index.shape[1]
     vm = pl.BlockSpec(memory_space=pltpu.VMEM)
     dma = pltpu.SemaphoreType.DMA
@@ -419,14 +446,14 @@
             pltpu.VMEM((8, pad_cells, LANES), F32),
             pltpu.VMEM((slots, pad_cells, LANES), F32),
             pltpu.VMEM((slots, hi_rows, obs), BF16),
-            pltpu.VMEM((slots, obs, 2 * LANES), BF16),
-            pltpu.VMEM((slots, -(-cells // 8) * 8, LANES), F32),
-            pltpu.VMEM((pad_cells, LANES), F32),
+            pltpu.VMEM((slots, obs, LANES), BF16),
+            pltpu.VMEM((slots, pad_cells, LANES), F32),
+            pltpu.VMEM((8, pad_cells, LANES), F32),
             pltpu.VMEM((n, pad_rows, LANES), BF16),
             pltpu.VMEM((n, pad_rows, LANES), BF16),
             pltpu.VMEM((2, LANES), F32),
             pltpu.VMEM((n, 2, LANES), F32),
-            dma, dma((n // 8,)), dma, dma, dma, dma,
+            dma, dma((n // 4,)), dma, dma, dma, dma,
         ],
         compiler_params=pltpu.CompilerParams(
             collective_id=0, has_side_effects=True, vmem_limit_bytes=24 << 20

time: 27.8 us -> 26.2 us (0.942)
  Pallas kernels: 27 us -> 25.4 us
    pallas_call x1, Pallas kernels: 26.3 us -> 24.7 us  [fused_device(): pl.pallas_call(functools.partial(step_kernel, nt, ns, len(sources)), out_...]
where the time goes in v3:
time: 26.2 us; the launch traced here: 26 us
  Pallas kernels  25.4 us (97%)
  between operations  0.64 us (2%)
    pallas_call x1, Pallas kernels, fused_device(): pl.pallas_call(functools.partial(step_kernel, nt, ns, len(sources)), out_...  24.7 us
    pallas_call x1, Pallas kernels, fused_device(): pl.pallas_call(put_kernel, out_shape=(jax.ShapeDtypeStruct((grid_rows, LA...  0.7 us

profile of v3, /device:TPU:0, one launch (start us, length us, event | category | flops | bytes accessed | tf_op | source)
XLA Modules:
  0.0 26.0 jit_solution(12468578983645092454)
XLA Ops:
  0.6 24.7 %envar_step.1 = (f32[400,128]{1,0:T(8,128)S(1)}, f32[1,128]{1,0:T(1,128)S(1)}) custom-call(f32[400,128]{1,0:T(8,128)} %bitcast.25, f32[400,128]{1,0:T(8,128)} %bitcast.26, bf16[160,160]{1,0:T(8,128)(2,1)} %constant.10.clone.refs_2_, bf16[320,320]{1,0:T(8,128)(2,1)} %constant.9.clone.refs_3_, s32[32,128]{1,0:T(8,128)} %bitcast.27, ...), custom_call_target="tpu_custom_call" | custom-call | tf_op jit(solution)/shard_map/envar_step/pallas_call | solution.py:432
  25.3 0.7 %put_results.1 = (f32[400,128]{1,0:T(8,128)}, f32[1,128]{1,0:T(1,128)}) custom-call(f32[400,128]{1,0:T(8,128)S(1)} %get-tuple-element.6.out, f32[1,128]{1,0:T(1,128)S(1)} %get-tuple-element.7.cost), custom_call_target="tpu_custom_call" | custom-call | tf_op jit(solution)/shard_map/put_results/pallas_call | solution.py:463

commit v4 on v3

--- a/solution.py
+++ b/solution.py
@@ -153,7 +153,9 @@
     group = 8
     bits = [lax.rem(lax.div(me, 1 << i), 2) for i in range(n.bit_length() - 1)]
     n_groups = n // group
-    ranges = [(16, rows - 16, sent - 16), (0, 16, 16)] if rows > 16 else [(0, rows, sent)]
+    cuts = (20, 10, 0) if rows > 20 else (0,)
+    ends = (rows,) + cuts[:-1]
+    ranges = [(a, b - a, b - a + (b - a) % 2) for a, b in zip(cuts, ends)]
 
     def device(peer):
         return (lax.div(peer, ns), lax.rem(peer, ns))
@@ -163,9 +165,6 @@
 
     def load(i):
         return pltpu.make_async_copy(sources[i], landed[i], in_sem.at[i])
-
-    for i in (0, 1, 2, 3, 4):
-        load(i).start()
 
     barrier = pltpu.get_barrier_semaphore()
 
@@ -173,6 +172,8 @@
         pl.semaphore_signal(
             barrier, inc=1, device_id=device(peer_of(k)), device_id_type=MESH_ID
         )
+    for i in (0, 1, 2, 3, 4):
+        load(i).start()
 
     def wide_of(ref):
         return jnp.concatenate(
@@ -245,6 +246,16 @@
 
     block_bits = bits[group.bit_length() - 1 :]
 
+    for i in (6, 7, 8):
+        load(i).wait()
+    models = [jnp.zeros((chunks, LANES), F32) for t in range(slots)]
+    known = []
+    for t in range(slots):
+        mine = pl.ds(t, chunks, stride=slots)
+        qct = qc[mine, :]
+        rad = jnp.where(qct == 0, 4.0, jnp.where(qct == 1, 2.0, 1.0)).astype(F32)
+        known.append((rad, 1.0 / (rad * rad), innov[mine, :], 1.0 / sigma[mine, :]))
+
     def add_group(p, g, own):
         r0, real, wide = ranges[p]
         at = pl.ds(r0 * levels, real * levels)
@@ -272,7 +283,6 @@
 
         lax.fori_loop(1, n_groups, next_group, 0)
 
-    models = [jnp.zeros((chunks, LANES), F32) for t in range(slots)]
     costs = [None] * slots
 
     def observe(p):
@@ -284,14 +294,11 @@
                     jnp.broadcast_to(table[t, h : h + 1, :], (chunks, LANES)), los[t]
                 )
                 models[t] = jnp.where(his[t] == h, picked, models[t])
-            mine = pl.ds(t, chunks, stride=slots)
-            sg = sigma[mine, :]
-            qct = qc[mine, :]
-            rad = jnp.where(qct == 0, 4.0, jnp.where(qct == 1, 2.0, 1.0)).astype(F32)
-            scaled = (models[t] - innov[mine, :]) / sg
-            sq = scaled * scaled / (rad * rad)
+            rad, bent, seen, inv = known[t]
+            scaled = (models[t] - seen) * inv
+            sq = scaled * scaled * bent
             costs[t] = (rad, sq)
-            g = scaled / ((1.0 + sq) * sg)
+            g = scaled * inv / (1.0 + sq)
             terms = jnp.concatenate(
                 [
                     hi_hot[t, r0 * levels : top, c * LANES : (c + 1) * LANES]
@@ -302,10 +309,10 @@
             )
             upd[t, r0 * levels : top, :] = mm(terms, lo_hot[t]).astype(BF16).astype(F32)
 
-    def a_copy(p, peer):
+    def a_copy(p, peer, far):
         at = pl.ds(ranges[p][0], ranges[p][2])
         return pltpu.make_async_remote_copy(
-            send_a.at[peer, at], recv_a.at[me, at], sa_sem, ra_sem,
+            send_a.at[peer, at], recv_a.at[me, at], sa_sem, ra_sem.at[far],
             device_id=device(peer), device_id_type=MESH_ID,
         )
 
@@ -323,32 +330,25 @@
         return sum((1 - 2 * b) * (1 << j) for j, b in enumerate(bits[:3]) if i >> j & 1)
 
     def adjoints(p):
-        def eight(d, before):
+        def eight(d, c):
             base = xor_of(block_bits, n_groups - 1 - d) * group + lax.rem(me, group)
-            for i in range(group - 1, -1, -1):
-                peer = base + low_of(i)
+            peers = [base + low_of(i) for i in range(group - 1, -1, -1)]
+            for i, peer in enumerate(peers):
                 one_member(p, peer, i, send_a.at[peer])
-                if i < group - 1:
-                    a_copy(p, base + low_of(i + 1)).start()
-            return base
-
-        def next_eight(d, before):
-            a_copy(p, before).start()
-            return eight(d, before)
-
-        last = lax.fori_loop(1, n_groups - 1, next_eight, eight(0, 0))
-        for i in range(group - 1, 0, -1):
-            peer = peer_of(i)
+            for peer in peers:
+                a_copy(p, peer, lax.rem(n_groups - 1 - d, 2)).start()
+            return c
+
+        lax.fori_loop(0, n_groups - 1, eight, 0)
+        peers = [peer_of(i) for i in range(group - 1, 0, -1)]
+        for i, peer in enumerate(peers):
             one_member(p, peer, i, send_a.at[peer])
-            a_copy(p, last if i == group - 1 else peer_of(i + 1)).start()
-        one_member(p, me, 0, recv_a.at[me])
-        a_copy(p, peer_of(1)).start()
+        one_member(p, me, group - 1, recv_a.at[me])
+        for peer in peers:
+            a_copy(p, peer, 0).start()
 
     for p in range(len(ranges)):
         increments(p)
-        if p == 0:
-            for i in (6, 7, 8):
-                load(i).wait()
         observe(p)
         adjoints(p)
 
@@ -359,12 +359,17 @@
     for i in (9, 10):
         load(i).wait()
 
-    others = recv_a.at[pl.ds(0, n - 1), pl.ds(0, sent)]
-    pltpu.make_async_copy(others, others, ra_sem).wait()
-    for s in range(ns):
-        flat[s * rows : (s + 1) * rows, :] = sum(
-            recv_a[t * ns + s].astype(F32)[:rows] for t in range(nt)
-        )
+    for far in (0, 1):
+        pieces = n // 2 - 1 + far
+        arrived = recv_a.at[pl.ds(0, pieces), pl.ds(0, sent)]
+        pltpu.make_async_copy(arrived, arrived, ra_sem.at[far]).wait()
+        half = lax.rem(block_bits[0] + far, 2)
+        for i in range(ns // 2):
+            s = half * (ns // 2) + i
+            at = pl.multiple_of(half * (ns // 2 * rows), 8) + i * rows
+            flat[pl.ds(at, rows), :] = sum(
+                recv_a[t * ns + s].astype(F32)[:rows] for t in range(nt)
+            )
     mid = mm(cxp[...], unfold(wide_of(flat).astype(BF16))).astype(BF16)
     gr = ctl + spec * fold(mm(mid, cyt[...]))
     sq = jnp.sum(gr * gr, axis=0, keepdims=True)
@@ -453,7 +458,7 @@
             pltpu.VMEM((n, pad_rows, LANES), BF16),
             pltpu.VMEM((2, LANES), F32),
             pltpu.VMEM((n, 2, LANES), F32),
-            dma, dma((n // 4,)), dma, dma, dma, dma,
+            dma, dma((3 * n // 8,)), dma, dma((2,)), dma, dma,
         ],
         compiler_params=pltpu.CompilerParams(
             collective_id=0, has_side_effects=True, vmem_limit_bytes=24 << 20

time: 26.2 us -> 25.8 us (0.985)
  Pallas kernels: 25.4 us -> 24.9 us
    pallas_call x1, Pallas kernels: 24.7 us -> 24.2 us  [fused_device(): pl.pallas_call(functools.partial(step_kernel, nt, ns, len(sources)), out_...]
where the time goes in v4:
time: 25.8 us; the launch traced here: 25.6 us
  Pallas kernels  24.9 us (97%)
  between operations  0.64 us (2%)
    pallas_call x1, Pallas kernels, fused_device(): pl.pallas_call(functools.partial(step_kernel, nt, ns, len(sources)), out_...  24.2 us
    pallas_call x1, Pallas kernels, fused_device(): pl.pallas_call(put_kernel, out_shape=(jax.ShapeDtypeStruct((grid_rows, LA...  0.7 us

profile of v4, /device:TPU:0, one launch (start us, length us, event | category | flops | bytes accessed | tf_op | source)
XLA Modules:
  0.0 25.6 jit_solution(2876006750241824201)
XLA Ops:
  0.6 24.2 %envar_step.1 = (f32[400,128]{1,0:T(8,128)S(1)}, f32[1,128]{1,0:T(1,128)S(1)}) custom-call(f32[400,128]{1,0:T(8,128)} %bitcast.25, f32[400,128]{1,0:T(8,128)} %bitcast.26, bf16[160,160]{1,0:T(8,128)(2,1)} %constant.10.clone.refs_2_, bf16[320,320]{1,0:T(8,128)(2,1)} %constant.9.clone.refs_3_, s32[32,128]{1,0:T(8,128)} %bitcast.27, ...), custom_call_target="tpu_custom_call" | custom-call | tf_op jit(solution)/shard_map/envar_step/pallas_call | solution.py:437
  24.9 0.7 %put_results.1 = (f32[400,128]{1,0:T(8,128)}, f32[1,128]{1,0:T(1,128)}) custom-call(f32[400,128]{1,0:T(8,128)S(1)} %get-tuple-element.6.out, f32[1,128]{1,0:T(1,128)S(1)} %get-tuple-element.7.cost), custom_call_target="tpu_custom_call" | custom-call | tf_op jit(solution)/shard_map/put_results/pallas_call | solution.py:468

commit v5 on v4

--- a/solution.py
+++ b/solution.py
@@ -153,7 +153,7 @@
     group = 8
     bits = [lax.rem(lax.div(me, 1 << i), 2) for i in range(n.bit_length() - 1)]
     n_groups = n // group
-    cuts = (20, 10, 0) if rows > 20 else (0,)
+    cuts = (20, 12, 0) if rows > 20 else (0,)
     ends = (rows,) + cuts[:-1]
     ranges = [(a, b - a, b - a + (b - a) % 2) for a, b in zip(cuts, ends)]
 
@@ -165,6 +165,9 @@
 
     def load(i):
         return pltpu.make_async_copy(sources[i], landed[i], in_sem.at[i])
+
+    for i in (0, 1, 2, 3):
+        load(i).start()
 
     barrier = pltpu.get_barrier_semaphore()
 
@@ -172,8 +175,7 @@
         pl.semaphore_signal(
             barrier, inc=1, device_id=device(peer_of(k)), device_id_type=MESH_ID
         )
-    for i in (0, 1, 2, 3, 4):
-        load(i).start()
+    load(4).start()
 
     def wide_of(ref):
         return jnp.concatenate(
@@ -392,7 +394,10 @@
     all_parts = parts.at[pl.ds(0, n - 1)]
     pltpu.make_async_copy(all_parts, all_parts, sp_sem).wait()
     pltpu.make_async_copy(all_parts, all_parts, rp_sem).wait()
-    sums = jnp.sum(jnp.sum(parts[...], axis=0), axis=1, keepdims=True)
+    sums = [parts[i] for i in range(n)]
+    while len(sums) > 1:
+        sums = [a + b for a, b in zip(sums[::2], sums[1::2])]
+    sums = jnp.sum(sums[0], axis=1, keepdims=True)
     total_cost, grad_sq = sums[0:1, :], sums[1:2, :]
     step = 0.5 * total_cost / (grad_sq + 1e-06)
     out[...] = control[...] - step * flat[: q * tiles, :]

time: 25.8 us -> 25.6 us (level)
  no operation moved by 1% of the time
where the time goes in v5:
time: 25.6 us; the launch traced here: 25.4 us
  Pallas kernels  24.8 us (97%)
  between operations  0.64 us (2%)
    pallas_call x1, Pallas kernels, fused_device(): pl.pallas_call(functools.partial(step_kernel, nt, ns, len(sources)), out_...  24.1 us
    pallas_call x1, Pallas kernels, fused_device(): pl.pallas_call(put_kernel, out_shape=(jax.ShapeDtypeStruct((grid_rows, LA...  0.7 us

profile of v5, /device:TPU:0, one launch (start us, length us, event | category | flops | bytes accessed | tf_op | source)
XLA Modules:
  0.0 25.4 jit_solution(5697227584671271828)
XLA Ops:
  0.6 24.1 %envar_step.1 = (f32[400,128]{1,0:T(8,128)S(1)}, f32[1,128]{1,0:T(1,128)S(1)}) custom-call(f32[400,128]{1,0:T(8,128)} %bitcast.25, f32[400,128]{1,0:T(8,128)} %bitcast.26, bf16[160,160]{1,0:T(8,128)(2,1)} %constant.10.clone.refs_2_, bf16[320,320]{1,0:T(8,128)(2,1)} %constant.9.clone.refs_3_, s32[32,128]{1,0:T(8,128)} %bitcast.27, ...), custom_call_target="tpu_custom_call" | custom-call | tf_op jit(solution)/shard_map/envar_step/pallas_call | solution.py:442
  24.7 0.7 %put_results.1 = (f32[400,128]{1,0:T(8,128)}, f32[1,128]{1,0:T(1,128)}) custom-call(f32[400,128]{1,0:T(8,128)S(1)} %get-tuple-element.6.out, f32[1,128]{1,0:T(1,128)S(1)} %get-tuple-element.7.cost), custom_call_target="tpu_custom_call" | custom-call | tf_op jit(solution)/shard_map/put_results/pallas_call | solution.py:473

commit v6 on v5

--- a/solution.py
+++ b/solution.py
@@ -153,7 +153,7 @@
     group = 8
     bits = [lax.rem(lax.div(me, 1 << i), 2) for i in range(n.bit_length() - 1)]
     n_groups = n // group
-    cuts = (20, 12, 0) if rows > 20 else (0,)
+    cuts = (20, 14, 0) if rows > 20 else (0,)
     ends = (rows,) + cuts[:-1]
     ranges = [(a, b - a, b - a + (b - a) % 2) for a, b in zip(cuts, ends)]
 

time: 25.6 us -> 25.6 us (level)
  no operation moved by 1% of the time
where the time goes in v6:
time: 25.6 us; the launch traced here: 25.4 us
  Pallas kernels  24.8 us (97%)
  between operations  0.64 us (2%)
    pallas_call x1, Pallas kernels, fused_device(): pl.pallas_call(functools.partial(step_kernel, nt, ns, len(sources)), out_...  24.1 us
    pallas_call x1, Pallas kernels, fused_device(): pl.pallas_call(put_kernel, out_shape=(jax.ShapeDtypeStruct((grid_rows, LA...  0.7 us

profile of v6, /device:TPU:0, one launch (start us, length us, event | category | flops | bytes accessed | tf_op | source)
XLA Modules:
  0.0 25.4 jit_solution(1456969256072770173)
XLA Ops:
  0.6 24.1 %envar_step.1 = (f32[400,128]{1,0:T(8,128)S(1)}, f32[1,128]{1,0:T(1,128)S(1)}) custom-call(f32[400,128]{1,0:T(8,128)} %bitcast.25, f32[400,128]{1,0:T(8,128)} %bitcast.26, bf16[160,160]{1,0:T(8,128)(2,1)} %constant.10.clone.refs_2_, bf16[320,320]{1,0:T(8,128)(2,1)} %constant.9.clone.refs_3_, s32[32,128]{1,0:T(8,128)} %bitcast.27, ...), custom_call_target="tpu_custom_call" | custom-call | tf_op jit(solution)/shard_map/envar_step/pallas_call | solution.py:442
  24.7 0.7 %put_results.1 = (f32[400,128]{1,0:T(8,128)}, f32[1,128]{1,0:T(1,128)}) custom-call(f32[400,128]{1,0:T(8,128)S(1)} %get-tuple-element.6.out, f32[1,128]{1,0:T(1,128)S(1)} %get-tuple-element.7.cost), custom_call_target="tpu_custom_call" | custom-call | tf_op jit(solution)/shard_map/put_results/pallas_call | solution.py:473
